TPU v7x, 32 devices: a whole 2x2x4 slice. The times are simulated.
32 devices in a mesh: groups: 2 (over y), expert: 4 (over z), tensor: 2 (over x), inner: 2 (over core).
Axes of the slice: x: 2, y: 2, z: 4, core: 2. Of those that a mesh axis runs over, the one named last changes fastest.
Arguments:
- tokens: bfloat16 [1024, 7168], P(('groups', 'expert'), ('tensor', 'inner')), parts along dimension 0, may hold values from -6 to 6
- expert_ids: int32 [1024, 8], P(('groups', 'expert')), parts along dimension 0, may hold values from 0 to 31, all different within a row; in each aligned block of 128 rows (0 to 127, 128 to 255, ...) at most 96 rows name the same one
- gate_weights: float32 [1024, 8], P(('groups', 'expert')), parts along dimension 0, may hold values from 0.05 to 0.45
- base_weights: bfloat16 [3, 1024, 7168], P(None, 'expert', ('tensor', 'inner')), may hold values from -0.0625 to 0.0625
- in_factor: bfloat16 [3840, 7168], P('expert', ('tensor', 'inner')), may hold values from -0.0625 to 0.0625
- out_factors: bfloat16 [2, 3840, 1024], P(None, 'expert', ('tensor', 'inner')), may hold values from -0.375 to 0.375
- ranks: int32 [32], P('expert'), may hold values from 64 to 512, as said below
Outputs:
- mixed: bfloat16 [1024, 7168], P(('groups', 'expert'), ('tensor', 'inner')), parts along dimension 0
There are 2 independent parts, one for each index of `groups`. A program takes and returns all parts, laid end to end along the dimension named above; an argument that names none is the same for every part. Nothing has to cross between parts.
Inputs may be any that keep to these rules, and one draw needn't show every extreme that they name: `expert_ids`: in each aligned block of 128 tokens no expert is chosen more than 96 times, and some expert is chosen exactly 96 times; the experts of one token differ. The ranks of each aligned block of 8 experts sum to exactly 960.
All inputs are finite; a program needn't handle non-finite values.
Results may differ from a plain program's by a relative error of at most 0.023.
Values may be sent and summed in bfloat16 or wider, within the bound.
No kernel may reach another device: no remote copies, remote signals or barrier semaphores. Data moves between devices by JAX's collectives and lax.ppermute only.
A program may use at most 64 MiB of HBM per device.

v0:
```python
import jax
import jax.numpy as jnp
from jax import lax
from jax.sharding import PartitionSpec as P

RANK_MAX = 512


def on_device(tokens, expert_ids, gate_weights, base_weights, in_factor, out_factors, ranks):
    tok_rows, feat_slice = tokens.shape
    top_count = expert_ids.shape[1]
    owners = lax.axis_size("expert")
    local_count = ranks.shape[0]
    experts = local_count * owners
    capacity = min(tok_rows, 3 * tok_rows * top_count // experts)
    hidden_slice = out_factors.shape[2]
    width = RANK_MAX
    gathered = lax.all_gather(base_weights, "expert", axis=1, tiled=True)
    partial_value = jnp.einsum(
        "td,gfd->tgf", tokens, gathered[:2], preferred_element_type=jnp.float32
    )
    base_rows = lax.psum_scatter(
        partial_value.astype(jnp.bfloat16), ("tensor", "inner"), scatter_dimension=2, tiled=True
    )
    pairs = tok_rows * top_count
    flat_ids = expert_ids.reshape(pairs)
    columns = lax.broadcasted_iota(jnp.int32, (pairs, experts), 1)
    onehot = (flat_ids[:, None] == columns).astype(jnp.bfloat16)
    row_pos = lax.broadcasted_iota(jnp.int32, (pairs, pairs), 0)
    col_pos = lax.broadcasted_iota(jnp.int32, (pairs, pairs), 1)
    earlier = (row_pos > col_pos).astype(jnp.bfloat16)
    counts = jnp.dot(earlier, onehot, preferred_element_type=jnp.float32)
    slot = jnp.sum(counts * onehot.astype(jnp.float32), axis=1).astype(jnp.int32)
    owner_of = flat_ids // local_count
    member_of = flat_ids % local_count
    target = (member_of * owners + owner_of) * capacity + slot
    source_row = lax.broadcasted_iota(jnp.int32, (pairs,), 0) // top_count
    outgoing = jnp.zeros((local_count * owners * capacity, feat_slice), jnp.bfloat16)
    outgoing = outgoing.at[target].set(tokens[source_row])
    outgoing = outgoing.reshape(local_count, owners, capacity, feat_slice)
    arrived = lax.all_to_all(outgoing, "expert", split_axis=1, concat_axis=1, tiled=True)
    slots = owners * capacity
    arrived = arrived.reshape(local_count, slots, feat_slice)
    starts = jnp.cumsum(ranks) - ranks
    in_pad = jnp.concatenate([in_factor, jnp.zeros((width, feat_slice), jnp.bfloat16)], 0)
    out_pad = jnp.concatenate([out_factors, jnp.zeros((2, width, hidden_slice), jnp.bfloat16)], 1)
    within = lax.broadcasted_iota(jnp.int32, (1, width), 1)
    terms = []
    for member in range(local_count):
        window = lax.dynamic_slice_in_dim(in_pad, starts[member], width, 0)
        terms.append(
            lax.dot_general(
                arrived[member],
                window,
                (((1,), (1,)), ((), ())),
                preferred_element_type=jnp.float32,
            )
        )
    stacked = jnp.stack(
        [
            jnp.where(within < ranks[member], terms[member], jnp.float32(0.0))
            for member in range(local_count)
        ]
    )
    summed = lax.psum(stacked.astype(jnp.bfloat16), ("tensor", "inner"))
    latents = [summed[member] for member in range(local_count)]
    outputs = []
    for member in range(local_count):
        factor = lax.dynamic_slice_in_dim(out_pad, starts[member], width, 1)
        outputs.append(
            jnp.einsum(
                "rc,gcf->rgf", latents[member], factor, preferred_element_type=jnp.float32
            ).astype(jnp.bfloat16)
        )
    replies = jnp.stack(outputs).reshape(local_count, owners, capacity, 2, hidden_slice)
    returned = lax.all_to_all(replies, "expert", split_axis=1, concat_axis=1, tiled=True)
    returned = returned.reshape(local_count * owners * capacity, 2, hidden_slice)
    delta = returned[target].reshape(tok_rows, top_count, 2, hidden_slice)
    summed_rows = base_rows.astype(jnp.float32)[:, None] + delta.astype(jnp.float32)
    hidden = (jax.nn.silu(summed_rows[:, :, 0]) * summed_rows[:, :, 1]).astype(jnp.bfloat16)
    combined = jnp.sum(gate_weights[:, :, None] * hidden.astype(jnp.float32), axis=1).astype(
        jnp.bfloat16
    )
    full_hidden = lax.all_gather(combined, ("tensor", "inner"), axis=1, tiled=True)
    return jnp.dot(full_hidden, gathered[2], preferred_element_type=jnp.float32).astype(
        jnp.bfloat16
    )


def solution(mesh):
    return jax.shard_map(
        on_device,
        mesh=mesh,
        in_specs=(
            P(("groups", "expert"), ("tensor", "inner")),
            P(("groups", "expert"), None),
            P(("groups", "expert"), None),
            P(None, "expert", ("tensor", "inner")),
            P("expert", ("tensor", "inner")),
            P(None, "expert", ("tensor", "inner")),
            P("expert"),
        ),
        out_specs=P(("groups", "expert"), ("tensor", "inner")),
        check_vma=False,
    )
```

profile of v0, /device:TPU:0, one launch (start us, length us, event | category | flops | bytes accessed | tf_op | source)
XLA Modules:
  0.0 655.1 jit_solution(18073991329550731420)
XLA Ops:
  9.0 31.3 %scatter_custom_fusion = bf16[3072,1792]{1,0:T(8,128)(2,1)} fusion(s32[1024]{0:T(1024)S(1)} %bitcast.155, bf16[]{:T(256)} %constant.47.clone.1, bf16[128,1792]{1,0:T(8,128)(2,1)S(1)} %copy-done, s32[1024]{0:T(1024)S(1)} %broadcast_clamp_fusion.1), kind=kCustom, calls=%fused_computation.13 | custom fusion | bytes 11010050 | tf_op jit(solution)/shard_map/scatter | solution.py:39
  40.3 9.6 %copy.42 = bf16[8,4,96,1792]{3,2,0,1:T(8,128)(2,1)} copy(bf16[8,4,96,1792]{3,2,1,0:T(8,128)(2,1)} %bitcast.135) | data formatting | bytes 22020096 | tf_op jit(solution)/shard_map/reshape | solution.py:40
  50.0 6.5 all-to-all-start
  78.2 218.9 %all-to-all-done = bf16[8,4,96,1792]{3,2,0,1:T(8,128)(2,1)} async-done(((bf16[8,4,96,1792]{3,2,0,1:T(8,128)(2,1)}), bf16[8,4,96,1792]{3,2,0,1:T(8,128)(2,1)}, u32[]{:S(2)}, u32[]{:S(2)}) %all-to-all-start) | async-done | bytes 11010080 | tf_op jit(solution)/shard_map/all_to_all | solution.py:41
  297.2 4.9 fusion.91
  302.4 1.9 fusion.50
  304.3 1.9 fusion.48
  306.2 1.9 fusion.46
  308.1 1.9 fusion.44
  310.0 1.9 fusion.42
  311.9 1.9 fusion.40
  313.8 1.9 fusion.38
  315.7 1.9 fusion.36
  318.2 67.2 %all-reduce.4.cloned.1.call-done = bf16[8,384,512]{2,1,0:T(8,128)(2,1)} async-done(((bf16[8,384,512]{2,1,0:T(8,128)(2,1)}), bf16[8,384,512]{2,1,0:T(8,128)(2,1)}) %all-reduce.4.cloned.1.call-update) | async-done | bytes 3145744 | tf_op jit(solution)/shard_map/psum | solution.py:65
  392.0 1.9 copy.54
  393.9 4.7 all-to-all-start.1
  398.6 179.9 %all-gather.2.cloned.1.call-done = bf16[3,1024,1792]{2,1,0:T(8,128)(2,1)} async-done(((bf16[3,256,1792]{2,1,0:T(8,128)(2,1)}), bf16[3,1024,1792]{2,1,0:T(8,128)(2,1)}) %all-gather.2.cloned.1.call-update) | async-done | bytes 11010064 | tf_op jit(solution)/shard_map/all_gather | solution.py:18
  578.4 6.3 fusion.16
  584.9 19.8 %reduce-scatter.2.cloned.1.call-done = bf16[128,2,256]{2,0,1:T(8,128)(2,1)} async-done(((bf16[128,2,1024]{2,0,1:T(8,128)(2,1)}), bf16[128,2,256]{2,0,1:T(8,128)(2,1)}) %reduce-scatter.2.cloned.1.call-update) | async-done | bytes 131088 | tf_op jit(solution)/shard_map/reduce_scatter | solution.py:22
  605.8 2.2 copy.51
  607.9 20.6 %copy.52 = bf16[3072,2,256]{2,1,0:T(2,128)(2,1)} copy(bf16[3072,2,256]{2,0,1:T(8,128)(2,1)S(1)} %bitcast.136) | data formatting | bytes 6291456 | tf_op jit(solution)/shard_map/reshape | solution.py:77
  628.5 6.1 gather_fusion
  638.1 5.8 all_gather.7
  643.8 3.5 fusion.7
  (60 shorter events, 20.2 us)
Async XLA Ops:
  7.4 1.7 copy-start
  50.0 6.5 copy-start.3
  50.0 247.2 %all-to-all-start = ((bf16[8,4,96,1792]{3,2,0,1:T(8,128)(2,1)}), bf16[8,4,96,1792]{3,2,0,1:T(8,128)(2,1)}, u32[]{:S(2)}, u32[]{:S(2)}) async-start(bf16[8,4,96,1792]{3,2,0,1:T(8,128)(2,1)} %copy.42), calls=%async_computation.1 | async-start | bytes 22020096 | tf_op jit(solution)/shard_map/all_to_all | solution.py:41
  56.5 329.0 %all-reduce.4.cloned.1.call-start = ((), (), s32[]{:S(2)}) async-start(), calls=%async_computation.5 | async-start | bytes 6291456 | tf_op jit(solution)/shard_map/psum | solution.py:65
  297.2 5.2 copy-start.5
  317.6 67.9 %copy-start.1 = (bf16[2,960,256]{2,1,0:T(8,128)(2,1)S(1)}, bf16[2,960,256]{2,1,0:T(8,128)(2,1)}, u32[]{:S(2)}) copy-start(bf16[2,960,256]{2,1,0:T(8,128)(2,1)} %param.12) | copy-start | bytes 2949124
  317.6 260.9 %all-gather.2.cloned.1.call-start = ((), (), s32[]{:S(2)}) async-start(), calls=%async_computation.3 | async-start | bytes 13762560 | tf_op jit(solution)/shard_map/all_gather | solution.py:18
  385.4 3.2 copy-start.2
  393.9 211.9 %all-to-all-start.1 = ((bf16[8,4,96,2,256]{4,2,0,3,1:T(8,128)(2,1)}), bf16[8,4,96,2,256]{4,2,0,3,1:T(8,128)(2,1)}, u32[]{:S(2)}, u32[]{:S(2)}) async-start(bf16[8,4,96,2,256]{4,2,0,3,1:T(8,128)(2,1)} %copy.54), calls=%async_computation.2 | async-start | bytes 6291456 | tf_op jit(solution)/shard_map/all_to_all | solution.py:76
  398.5 186.3 %copy-start.4 = (f32[128,8]{0,1:T(8,128)S(1)}, f32[128,8]{0,1:T(8,128)}, u32[]{:S(2)}) copy-start(f32[128,8]{0,1:T(8,128)} %param.9) | copy-start | bytes 12292
  398.5 206.2 %reduce-scatter.2.cloned.1.call-start = ((), (), s32[]{:S(2)}) async-start(), calls=%async_computation.4 | async-start | bytes 655360 | tf_op jit(solution)/shard_map/reduce_scatter | solution.py:22
Sparse Core Ops, SparseCore 0:
  317.7 67.6 all-reduce.3
  584.9 19.7 reduce-scatter.1
Sparse Core Ops, SparseCore 1:
  319.6 258.7 all-gather.1
where the time goes:
time: 664 us; the launch traced here: 655 us
  waiting for transfers between devices  486 us (73%)
  local copies, waits for them, and re-layouts  82.2 us (12%)
  matrix products  31.7 us (5%)
  between operations  30.7 us (5%)
  starting transfers between devices  11.4 us (2%)
  other arithmetic  7.15 us (1%)
    all_to_all x1, waiting for transfers between devices, on_device(): lax.all_to_all(outgoing, 'expert', split_axis=1, concat_axis=1, tiled=True)  219 us
    all_gather x1, waiting for transfers between devices, on_device(): gathered = lax.all_gather(base_weights, 'expert', axis=1, tiled=True)  180 us
    psum x1, waiting for transfers between devices, on_device(): summed = lax.psum(stacked.astype(jnp.bfloat16), ('tensor', 'inner'))  67.2 us
    scatter x1, local copies, waits for them, and re-layouts, on_device(): outgoing = outgoing.at[target].set(tokens[source_row])  31.3 us
    reshape x1, local copies, waits for them, and re-layouts, on_device(): returned.reshape(local_count * owners * capacity, 2, hidden_slice)  20.6 us
    reduce_scatter x1, waiting for transfers between devices, on_device(): lax.psum_scatter(partial_value.astype(jnp.bfloat16), ('tensor', 'inner'),...  19.8 us
    dot_general x8, matrix products, on_device(): lax.dot_general(arrived[member], window, (((1,), (1,)), ((), ())), prefer...  15.2 us
  transfers between devices with their start and end apart: 5, of which 4 were waited for; matrix products, arithmetic and copies ran while one was open for 3% of the time, Pallas kernels for 0%

commit v1 on v0

--- a/solution.py
+++ b/solution.py
@@ -2,11 +2,18 @@
 import jax.numpy as jnp
 from jax import lax
 from jax.sharding import PartitionSpec as P
+from jax.lax import psum
 
 RANK_MAX = 512
 
 
 def on_device(tokens, expert_ids, gate_weights, base_weights, in_factor, out_factors, ranks):
+
+    def lift_sizes(array_here, lane_axis, along_axis):
+        for i0 in (lane_axis, along_axis):
+            array_here = psum(array_here, i0)
+        return array_here
+
     tok_rows, feat_slice = tokens.shape
     top_count = expert_ids.shape[1]
     owners = lax.axis_size("expert")
@@ -62,7 +69,7 @@
             for member in range(local_count)
         ]
     )
-    summed = lax.psum(stacked.astype(jnp.bfloat16), ("tensor", "inner"))
+    summed = lift_sizes(stacked.astype(jnp.bfloat16), "inner", "tensor")
     latents = [summed[member] for member in range(local_count)]
     outputs = []
     for member in range(local_count):

time: 664 us -> 689 us (1.038)
  waiting for transfers between devices: 486 us -> 511 us
    psum x1 -> x2, waiting for transfers between devices: 67.2 us -> 111 us  [lift_sizes(): array_here = psum(array_here, i0)]
    all_gather x1, waiting for transfers between devices: 180 us -> 160 us  [on_device(): gathered = lax.all_gather(base_weights, 'expert', axis=1, tiled=True)]
  transfers between devices with their start and end apart: 5 -> 6, of which waited for: 4 -> 5; matrix products, arithmetic and copies ran while one was open for 3% -> 3% of each run, Pallas kernels for 0% -> 0%
where the time goes in v1:
time: 689 us; the launch traced here: 680 us
  waiting for transfers between devices  511 us (74%)
  local copies, waits for them, and re-layouts  82.2 us (12%)
  matrix products  31.7 us (5%)
  between operations  30.7 us (4%)
  starting transfers between devices  11.4 us (2%)
  other arithmetic  7.15 us (1%)
    all_to_all x1, waiting for transfers between devices, on_device(): lax.all_to_all(outgoing, 'expert', split_axis=1, concat_axis=1, tiled=True)  219 us
    all_gather x1, waiting for transfers between devices, on_device(): gathered = lax.all_gather(base_weights, 'expert', axis=1, tiled=True)  160 us
    psum x2, waiting for transfers between devices, lift_sizes(): array_here = psum(array_here, i0)  111 us
    scatter x1, local copies, waits for them, and re-layouts, on_device(): outgoing = outgoing.at[target].set(tokens[source_row])  31.3 us
    reshape x1, local copies, waits for them, and re-layouts, on_device(): returned.reshape(local_count * owners * capacity, 2, hidden_slice)  20.6 us
    reduce_scatter x1, waiting for transfers between devices, on_device(): lax.psum_scatter(partial_value.astype(jnp.bfloat16), ('tensor', 'inner'),...  19.7 us
    dot_general x8, matrix products, on_device(): lax.dot_general(arrived[member], window, (((1,), (1,)), ((), ())), prefer...  15.2 us
  transfers between devices with their start and end apart: 6, of which 5 were waited for; matrix products, arithmetic and copies ran while one was open for 3% of the time, Pallas kernels for 0%

profile of v1, /device:TPU:0, one launch (start us, length us, event | category | flops | bytes accessed | tf_op | source)
XLA Modules:
  0.0 679.8 jit_solution(12677376309301847689)
XLA Ops:
  9.0 31.3 %scatter_custom_fusion = bf16[3072,1792]{1,0:T(8,128)(2,1)} fusion(s32[1024]{0:T(1024)S(1)} %bitcast.155, bf16[]{:T(256)} %constant.47.clone.1, bf16[128,1792]{1,0:T(8,128)(2,1)S(1)} %copy-done, s32[1024]{0:T(1024)S(1)} %broadcast_clamp_fusion.1), kind=kCustom, calls=%fused_computation.13 | custom fusion | bytes 11010050 | tf_op jit(solution)/shard_map/scatter | solution.py:46
  40.4 9.6 %copy.42 = bf16[8,4,96,1792]{3,2,0,1:T(8,128)(2,1)} copy(bf16[8,4,96,1792]{3,2,1,0:T(8,128)(2,1)} %bitcast.135) | data formatting | bytes 22020096 | tf_op jit(solution)/shard_map/reshape | solution.py:47
  50.0 6.5 all-to-all-start
  78.3 218.9 %all-to-all-done = bf16[8,4,96,1792]{3,2,0,1:T(8,128)(2,1)} async-done(((bf16[8,4,96,1792]{3,2,0,1:T(8,128)(2,1)}), bf16[8,4,96,1792]{3,2,0,1:T(8,128)(2,1)}, u32[]{:S(2)}, u32[]{:S(2)}) %all-to-all-start) | async-done | bytes 11010080 | tf_op jit(solution)/shard_map/all_to_all | solution.py:48
  297.2 4.9 fusion.91
  302.4 1.9 fusion.50
  304.3 1.9 fusion.48
  306.2 1.9 fusion.46
  308.1 1.9 fusion.44
  310.0 1.9 fusion.42
  311.9 1.9 fusion.40
  315.7 1.9 fusion.36
  317.7 22.7 %all-reduce.5.cloned.1.call-done = bf16[8,384,512]{2,1,0:T(8,128)(2,1)} async-done(((bf16[8,384,512]{2,1,0:T(8,128)(2,1)}), bf16[8,384,512]{2,1,0:T(8,128)(2,1)}) %all-reduce.5.cloned.1.call-update) | async-done | bytes 3145744 | tf_op jit(solution)/shard_map/psum | solution.py:14
  340.9 88.7 %all-reduce.7.cloned.1.call-done = bf16[8,384,512]{2,1,0:T(8,128)(2,1)} async-done(((bf16[8,384,512]{2,1,0:T(8,128)(2,1)}), bf16[8,384,512]{2,1,0:T(8,128)(2,1)}) %all-reduce.7.cloned.1.call-update) | async-done | bytes 3145744 | tf_op jit(solution)/shard_map/psum | solution.py:14
  436.2 1.9 copy.54
  438.1 4.7 all-to-all-start.1
  442.8 160.3 %all-gather.2.cloned.1.call-done = bf16[3,1024,1792]{2,1,0:T(8,128)(2,1)} async-done(((bf16[3,256,1792]{2,1,0:T(8,128)(2,1)}), bf16[3,1024,1792]{2,1,0:T(8,128)(2,1)}) %all-gather.2.cloned.1.call-update) | async-done | bytes 11010064 | tf_op jit(solution)/shard_map/all_gather | solution.py:25
  603.2 6.3 fusion.16
  609.6 19.7 %reduce-scatter.2.cloned.1.call-done = bf16[128,2,256]{2,0,1:T(8,128)(2,1)} async-done(((bf16[128,2,1024]{2,0,1:T(8,128)(2,1)}), bf16[128,2,256]{2,0,1:T(8,128)(2,1)}) %reduce-scatter.2.cloned.1.call-update) | async-done | bytes 131088 | tf_op jit(solution)/shard_map/reduce_scatter | solution.py:29
  630.4 2.2 copy.51
  632.6 20.6 %copy.52 = bf16[3072,2,256]{2,1,0:T(2,128)(2,1)} copy(bf16[3072,2,256]{2,0,1:T(8,128)(2,1)S(1)} %bitcast.136) | data formatting | bytes 6291456 | tf_op jit(solution)/shard_map/reshape | solution.py:84
  653.2 6.1 gather_fusion
  662.7 5.8 all_gather.7
  668.5 3.5 fusion.7
  (63 shorter events, 22.1 us)
Async XLA Ops:
  7.4 1.7 copy-start
  50.0 6.5 copy-start.3
  50.0 247.2 %all-to-all-start = ((bf16[8,4,96,1792]{3,2,0,1:T(8,128)(2,1)}), bf16[8,4,96,1792]{3,2,0,1:T(8,128)(2,1)}, u32[]{:S(2)}, u32[]{:S(2)}) async-start(bf16[8,4,96,1792]{3,2,0,1:T(8,128)(2,1)} %copy.42), calls=%async_computation.1 | async-start | bytes 22020096 | tf_op jit(solution)/shard_map/all_to_all | solution.py:48
  56.5 283.8 %all-reduce.5.cloned.1.call-start = ((), (), s32[]{:S(2)}) async-start(), calls=%async_computation.5 | async-start | bytes 6291456 | tf_op jit(solution)/shard_map/psum | solution.py:14
  297.2 5.2 copy-start.5
  317.6 112.0 %copy-start.1 = (bf16[2,960,256]{2,1,0:T(8,128)(2,1)S(1)}, bf16[2,960,256]{2,1,0:T(8,128)(2,1)}, u32[]{:S(2)}) copy-start(bf16[2,960,256]{2,1,0:T(8,128)(2,1)} %param.12) | copy-start | bytes 2949124
  317.6 112.0 %all-reduce.7.cloned.1.call-start = ((), (), s32[]{:S(2)}) async-start(), calls=%async_computation.6 | async-start | bytes 6291456 | tf_op jit(solution)/shard_map/psum | solution.py:14
  340.4 262.8 %all-gather.2.cloned.1.call-start = ((), (), s32[]{:S(2)}) async-start(), calls=%async_computation.3 | async-start | bytes 13762560 | tf_op jit(solution)/shard_map/all_gather | solution.py:25
  429.7 3.2 copy-start.2
  438.1 192.3 %all-to-all-start.1 = ((bf16[8,4,96,2,256]{4,2,0,3,1:T(8,128)(2,1)}), bf16[8,4,96,2,256]{4,2,0,3,1:T(8,128)(2,1)}, u32[]{:S(2)}, u32[]{:S(2)}) async-start(bf16[8,4,96,2,256]{4,2,0,3,1:T(8,128)(2,1)} %copy.54), calls=%async_computation.2 | async-start | bytes 6291456 | tf_op jit(solution)/shard_map/all_to_all | solution.py:83
  442.8 166.7 %copy-start.4 = (f32[128,8]{0,1:T(8,128)S(1)}, f32[128,8]{0,1:T(8,128)}, u32[]{:S(2)}) copy-start(f32[128,8]{0,1:T(8,128)} %param.9) | copy-start | bytes 12292
  442.8 186.6 %reduce-scatter.2.cloned.1.call-start = ((), (), s32[]{:S(2)}) async-start(), calls=%async_computation.4 | async-start | bytes 655360 | tf_op jit(solution)/shard_map/reduce_scatter | solution.py:29
Sparse Core Ops, SparseCore 0:
  317.7 22.5 all-reduce.4
  342.6 86.9 all-reduce.6
Sparse Core Ops, SparseCore 1:
  342.4 260.7 all-gather.1
  609.6 19.7 reduce-scatter.1
